TPU v7x, 32 devices: a whole 2x2x4 slice. The times are simulated.
32 devices in a mesh: groups: 2 (over y), seq: 4 (over z), rep: 2 (over x), fsdp: 2 (over core).
Axes of the slice: x: 2, y: 2, z: 4, core: 2. Of those that a mesh axis runs over, the one named last changes fastest.
Arguments:
- activations: bfloat16 [8, 512, 2048], P(('groups', 'rep', 'fsdp'), 'seq'), parts along dimension 0, may hold values from -6 to 6
- queries: bfloat16 [8, 512, 2048], P(('groups', 'rep', 'fsdp'), 'seq'), parts along dimension 0, may hold values from -102 to 102
- key_weight: bfloat16 [2048, 512], P(('seq', 'fsdp')), may hold values from -0.125 to 0.125
- value_weight: bfloat16 [2048, 512], P(('seq', 'fsdp')), may hold values from -0.125 to 0.125
- segment_ids: int32 [8, 512], P(('groups', 'rep', 'fsdp'), 'seq'), parts along dimension 0, may hold values from 0 to 3, never falling along the last dimension, each value on 1 to 384 neighbouring positions
- out_grad: bfloat16 [8, 512, 2048], P(('groups', 'rep', 'fsdp'), 'seq'), parts along dimension 0, may hold values from -6 to 6
Outputs:
- context: bfloat16 [8, 512, 2048], P(('groups', 'rep', 'fsdp'), 'seq'), parts along dimension 0
- query_grad: bfloat16 [8, 512, 2048], P(('groups', 'rep', 'fsdp'), 'seq'), parts along dimension 0
- input_grad: bfloat16 [8, 512, 2048], P(('groups', 'rep', 'fsdp'), 'seq'), parts along dimension 0
- key_weight_grad: bfloat16 [4096, 512], P(('groups', 'seq', 'fsdp')), parts along dimension 0
- value_weight_grad: bfloat16 [4096, 512], P(('groups', 'seq', 'fsdp')), parts along dimension 0
There are 2 independent parts, one for each index of `groups`. A program takes and returns all parts, laid end to end along the dimension named above; an argument that names none is the same for every part. Nothing has to cross between parts.
Inputs may be any that keep to these rules, and one draw needn't show every extreme that they name: `segment_ids`: document numbers never fall along a sequence; a document covers at most 384 positions.
All inputs are finite; a program needn't handle non-finite values.
Results may differ from a plain program's by a relative error of at most 0.025.
The roundings to bfloat16 on the way count: a program that leaves them out, or rounds other values in their place, can miss the bound.
Values may be sent and summed in bfloat16 or wider, within the bound.
No kernel may reach another device: no remote copies, remote signals or barrier semaphores. Data moves between devices by JAX's collectives and lax.ppermute only.
A program may use at most 64 MiB of HBM per device.

v0:
```python
import math
import jax
import jax.numpy as jnp
from jax import lax
from jax.sharding import PartitionSpec as P

HEADS = 16
KV_HEADS = 4
HEAD_DIM = 128
masked_low = -1e30


def block_mask(seg_all, row_start, col_start, block_width):
    row_pos = row_start + lax.iota(jnp.int32, block_width)
    col_pos = col_start + lax.iota(jnp.int32, block_width)
    seg_rows = lax.dynamic_slice_in_dim(seg_all, row_start, block_width)
    seg_cols = lax.dynamic_slice_in_dim(seg_all, col_start, block_width)
    return (col_pos[None, :] <= row_pos[:, None]) & (seg_cols[None, :] == seg_rows[:, None])


def block_scores(query_block, key_block, inv_root):
    return (
        jnp.einsum("qhd,khd->hqk", query_block, key_block, preferred_element_type=jnp.float32)
        * inv_root
    )


def take_block(source, index, block_width):
    return lax.dynamic_slice_in_dim(source, index * block_width, block_width, 0)


def attend(query_part, key_part, value_part, seg_all):
    length, heads_here, head_size = query_part.shape
    block_width = min(512, length)
    block_count = length // block_width
    inv_root = 1.0 / math.sqrt(head_size)

    def stats_row(i, log_totals):
        query_block = take_block(query_part, i, block_width)

        def stats_inner(j, state_now):
            running_max, running_sum = state_now
            scores = block_scores(query_block, take_block(key_part, j, block_width), inv_root)
            allowed = block_mask(seg_all, i * block_width, j * block_width, block_width)[None]
            scores = jnp.where(allowed, scores, masked_low)
            new_max = jnp.maximum(running_max, jnp.max(scores, axis=-1))
            weights = jnp.where(allowed, jnp.exp(scores - new_max[..., None]), 0.0)
            running_sum = running_sum * jnp.exp(running_max - new_max) + jnp.sum(weights, axis=-1)
            return (new_max, running_sum)

        start_state = (
            jnp.full((heads_here, block_width), masked_low, jnp.float32),
            jnp.zeros((heads_here, block_width), jnp.float32),
        )
        running_max, running_sum = lax.fori_loop(0, i + 1, stats_inner, start_state)
        return lax.dynamic_update_slice_in_dim(
            log_totals, running_max + jnp.log(running_sum), i * block_width, 1
        )

    log_totals = lax.fori_loop(
        0, block_count, stats_row, jnp.zeros((heads_here, length), jnp.float32)
    )

    def out_row(i, out_all):
        query_block = take_block(query_part, i, block_width)
        log_block = lax.dynamic_slice_in_dim(log_totals, i * block_width, block_width, 1)

        def out_inner(j, accum_out):
            scores = block_scores(query_block, take_block(key_part, j, block_width), inv_root)
            allowed = block_mask(seg_all, i * block_width, j * block_width, block_width)[None]
            probs_low = jnp.where(allowed, jnp.exp(scores - log_block[..., None]), 0.0).astype(
                jnp.bfloat16
            )
            return accum_out + jnp.einsum(
                "hqk,khd->qhd",
                probs_low,
                take_block(value_part, j, block_width),
                preferred_element_type=jnp.float32,
            )

        accum_out = lax.fori_loop(
            0, i + 1, out_inner, jnp.zeros((block_width, heads_here, head_size), jnp.float32)
        )
        return lax.dynamic_update_slice_in_dim(
            out_all, accum_out.astype(jnp.bfloat16), i * block_width, 0
        )

    out_all = lax.fori_loop(
        0, block_count, out_row, jnp.zeros((length, heads_here, head_size), jnp.bfloat16)
    )
    return (out_all, log_totals)


def attend_grads(query_part, key_part, value_part, seg_all, out_part, log_totals, grad_part):
    length, heads_here, head_size = query_part.shape
    block_width = min(512, length)
    block_count = length // block_width
    inv_root = 1.0 / math.sqrt(head_size)
    row_dots = jnp.einsum("qhd,qhd->hq", grad_part, out_part, preferred_element_type=jnp.float32)

    def grad_row(i, state_now):
        query_all, key_all, value_all = state_now
        query_block = take_block(query_part, i, block_width)
        grad_block = take_block(grad_part, i, block_width)
        log_block = lax.dynamic_slice_in_dim(log_totals, i * block_width, block_width, 1)
        dots_block = lax.dynamic_slice_in_dim(row_dots, i * block_width, block_width, 1)

        def grad_inner(j, inner_state):
            query_accum, key_accum, value_accum = inner_state
            key_block = take_block(key_part, j, block_width)
            value_block = take_block(value_part, j, block_width)
            scores = block_scores(query_block, key_block, inv_root)
            allowed = block_mask(seg_all, i * block_width, j * block_width, block_width)[None]
            probs = jnp.where(allowed, jnp.exp(scores - log_block[..., None]), 0.0)
            probs_low = probs.astype(jnp.bfloat16)
            value_new = take_block(value_accum, j, block_width) + jnp.einsum(
                "hqk,qhd->khd", probs_low, grad_block, preferred_element_type=jnp.float32
            )
            value_accum = lax.dynamic_update_slice_in_dim(
                value_accum, value_new, j * block_width, 0
            )
            prob_grad = jnp.einsum(
                "qhd,khd->hqk", grad_block, value_block, preferred_element_type=jnp.float32
            )
            score_grad = (probs * (prob_grad - dots_block[..., None])).astype(jnp.bfloat16)
            query_accum = query_accum + jnp.einsum(
                "hqk,khd->qhd", score_grad, key_block, preferred_element_type=jnp.float32
            )
            key_new = take_block(key_accum, j, block_width) + jnp.einsum(
                "hqk,qhd->khd", score_grad, query_block, preferred_element_type=jnp.float32
            )
            key_accum = lax.dynamic_update_slice_in_dim(key_accum, key_new, j * block_width, 0)
            return (query_accum, key_accum, value_accum)

        start_state = (
            jnp.zeros((block_width, heads_here, head_size), jnp.float32),
            key_all,
            value_all,
        )
        query_accum, key_all, value_all = lax.fori_loop(0, i + 1, grad_inner, start_state)
        query_all = lax.dynamic_update_slice_in_dim(
            query_all, (query_accum * inv_root).astype(jnp.bfloat16), i * block_width, 0
        )
        return (query_all, key_all, value_all)

    zero_grads = jnp.zeros((length, heads_here, head_size), jnp.float32)
    start_all = (jnp.zeros((length, heads_here, head_size), jnp.bfloat16), zero_grads, zero_grads)
    query_all, key_all, value_all = lax.fori_loop(0, block_count, grad_row, start_all)
    return (query_all, (key_all * inv_root).astype(jnp.bfloat16), value_all.astype(jnp.bfloat16))


def body(activations, queries, key_weight, value_weight, segment_ids, out_grad):
    rows_here = activations.shape[1]
    inputs = activations[0]
    kv_width = key_weight.shape[1]
    seq_devices = lax.axis_size("seq")
    heads_here = HEADS // seq_devices
    kv_group = HEADS // KV_HEADS
    stacked = jnp.concatenate([key_weight, value_weight], axis=1)
    columns = inputs
    projected = jnp.dot(
        columns,
        lax.all_gather(stacked, ("seq", "fsdp"), axis=0, tiled=True),
        preferred_element_type=jnp.float32,
    )
    projected = projected.astype(jnp.bfloat16)
    key_rows = projected[:, :kv_width].reshape(rows_here, KV_HEADS, HEAD_DIM)
    value_rows = projected[:, kv_width:].reshape(rows_here, KV_HEADS, HEAD_DIM)
    kv_copies = max(kv_group // heads_here, 1)
    query_heads = queries[0].reshape(rows_here, HEADS, HEAD_DIM)
    sent = (
        query_heads,
        jnp.repeat(key_rows, kv_copies, axis=1),
        jnp.repeat(value_rows, kv_copies, axis=1),
    )
    query_part, key_part, value_part = (
        lax.all_to_all(sent[0], "seq", split_axis=1, concat_axis=0, tiled=True),
        lax.all_to_all(sent[1], "seq", split_axis=1, concat_axis=0, tiled=True),
        lax.all_to_all(sent[2], "seq", split_axis=1, concat_axis=0, tiled=True),
    )
    widen_by = heads_here // key_part.shape[1]
    key_part = jnp.repeat(key_part, widen_by, axis=1)
    value_part = jnp.repeat(value_part, widen_by, axis=1)
    seg_all = lax.all_gather(segment_ids[0], "seq", axis=0, tiled=True)
    out_part, log_totals = attend(query_part, key_part, value_part, seg_all)
    context = lax.all_to_all(out_part, "seq", split_axis=0, concat_axis=1, tiled=True).reshape(
        1, rows_here, HEADS * HEAD_DIM
    )
    grad_part = lax.all_to_all(
        out_grad[0].reshape(rows_here, HEADS, HEAD_DIM),
        "seq",
        split_axis=1,
        concat_axis=0,
        tiled=True,
    )
    query_back, key_back, value_back = attend_grads(
        query_part, key_part, value_part, seg_all, out_part, log_totals, grad_part
    )
    query_tok, key_tok, value_tok = (
        lax.all_to_all(query_back, "seq", split_axis=0, concat_axis=1, tiled=True),
        lax.all_to_all(key_back, "seq", split_axis=0, concat_axis=1, tiled=True),
        lax.all_to_all(value_back, "seq", split_axis=0, concat_axis=1, tiled=True),
    )
    key_sum = (
        key_tok.reshape(rows_here, KV_HEADS, kv_group, HEAD_DIM).astype(jnp.float32).sum(axis=2)
    )
    value_sum = (
        value_tok.reshape(rows_here, KV_HEADS, kv_group, HEAD_DIM).astype(jnp.float32).sum(axis=2)
    )
    grad_kv = jnp.concatenate(
        [
            key_sum.astype(jnp.bfloat16).reshape(rows_here, kv_width),
            value_sum.astype(jnp.bfloat16).reshape(rows_here, kv_width),
        ],
        axis=1,
    )
    input_grad = lax.dot_general(
        grad_kv,
        lax.all_gather(stacked, ("seq", "fsdp"), axis=0, tiled=True),
        (((1,), (1,)), ((), ())),
        preferred_element_type=jnp.float32,
    )
    input_grad = input_grad.astype(jnp.bfloat16).reshape(1, rows_here, inputs.shape[1])
    columns = inputs
    grad_shard = lax.psum_scatter(
        lax.dot_general(
            columns, grad_kv, (((0,), (0,)), ((), ())), preferred_element_type=jnp.float32
        ).astype(jnp.bfloat16),
        ("seq", "fsdp"),
        scatter_dimension=0,
        tiled=True,
    ).astype(jnp.float32)
    grad_total = lax.psum(grad_shard, "rep").astype(jnp.bfloat16)
    query_grad = query_tok.reshape(1, rows_here, HEADS * HEAD_DIM)
    return (context, query_grad, input_grad, grad_total[:, :kv_width], grad_total[:, kv_width:])


def solution(mesh):
    return jax.shard_map(
        body,
        mesh=mesh,
        in_specs=(
            P(("groups", "rep", "fsdp"), "seq", None),
            P(("groups", "rep", "fsdp"), "seq", None),
            P(("seq", "fsdp"), None),
            P(("seq", "fsdp"), None),
            P(("groups", "rep", "fsdp"), "seq"),
            P(("groups", "rep", "fsdp"), "seq", None),
        ),
        out_specs=(
            P(("groups", "rep", "fsdp"), "seq", None),
            P(("groups", "rep", "fsdp"), "seq", None),
            P(("groups", "rep", "fsdp"), "seq", None),
            P(("groups", "seq", "fsdp"), None),
            P(("groups", "seq", "fsdp"), None),
        ),
        check_vma=False,
    )
```

profile of v0, /device:TPU:0, one launch (start us, length us, event | category | flops | bytes accessed | tf_op | source)
XLA Modules:
  0.0 248.5 jit_solution(1533762481953320926)
XLA Ops:
  7.2 1.9 pad_maximum_fusion
  9.2 2.0 copy.45
  11.2 6.3 %all-to-all-start.1 = ((bf16[128,16,128]{0,2,1:T(8,128)(2,1)}), bf16[128,16,128]{0,2,1:T(8,128)(2,1)S(1)}, u32[]{:S(2)}, u32[]{:S(2)}) async-start(bf16[128,16,128]{0,2,1:T(8,128)(2,1)} %bitcast.9), calls=%async_computation.1 | async-start | bytes 1048576 | tf_op jit(solution)/shard_map/all_to_all | solution.py:177
  17.5 2.0 copy.52
  19.6 24.7 %all-to-all-done.1 = bf16[128,16,128]{0,2,1:T(8,128)(2,1)S(1)} async-done(((bf16[128,16,128]{0,2,1:T(8,128)(2,1)}), bf16[128,16,128]{0,2,1:T(8,128)(2,1)S(1)}, u32[]{:S(2)}, u32[]{:S(2)}) %all-to-all-start.1) | async-done | bytes 524320 | tf_op jit(solution)/shard_map/all_to_all | solution.py:177
  44.2 3.6 %all-to-all-start.4 = ((bf16[128,16,128]{0,2,1:T(8,128)(2,1)}), bf16[128,16,128]{0,2,1:T(8,128)(2,1)S(1)}, u32[]{:S(2)}, u32[]{:S(2)}) async-start(bf16[128,16,128]{0,2,1:T(8,128)(2,1)} %bitcast.22), calls=%async_computation.4 | async-start | bytes 1048576 | tf_op jit(solution)/shard_map/all_to_all | solution.py:189
  47.9 21.7 %all-gather = s32[1,512]{1,0:T(1,128)S(1)} all-gather(s32[1,128]{1,0:T(1,128)S(1)} %copy-done.3), channel_id=2, replica_groups=mesh['groups'=2,'seq'=4,'rep'=2,'fsdp'=2] {'seq'}, dimensions={1}, use_global_device_ids=true | all-gather | bytes 2560 | tf_op jit(solution)/shard_map/all_gather | solution.py:184
  69.5 9.1 %all-gather.3.cloned.1.call-done = bf16[2048,1024]{1,0:T(8,128)(2,1)} async-done(((bf16[256,1024]{1,0:T(8,128)(2,1)}), bf16[2048,1024]{1,0:T(8,128)(2,1)}) %all-gather.3.cloned.1.call-update) | async-done | bytes 4194320 | tf_op jit(solution)/shard_map/all_gather | solution.py:163
  78.7 3.5 %fusion.11 = bf16[128,1024]{0,1:T(8,128)(2,1)S(1)} fusion(bf16[2048,1024]{1,0:T(8,128)(2,1)} %all-gather.3.cloned.1.call-done, bf16[1,128,2048]{2,1,0:T(8,128)(2,1)S(1)} %copy-done), kind=kOutput, calls=%fused_computation.22 | convolution fusion | flops 537001984 | bytes 4980736 | tf_op jit(solution)/shard_map/dot_general | solution.py:161
  83.0 3.3 %all-to-all-start = ((bf16[128,4,128]{2,0,1:T(8,128)(2,1)}), bf16[128,4,128]{2,0,1:T(8,128)(2,1)S(1)}, u32[]{:S(2)}, u32[]{:S(2)}) async-start(bf16[128,4,128]{2,0,1:T(8,128)(2,1)} %copy.44), calls=%async_computation | async-start | bytes 262144 | tf_op jit(solution)/shard_map/all_to_all | solution.py:178
  87.9 4.8 %all-to-all-done = bf16[128,4,128]{2,0,1:T(8,128)(2,1)S(1)} async-done(((bf16[128,4,128]{2,0,1:T(8,128)(2,1)}), bf16[128,4,128]{2,0,1:T(8,128)(2,1)S(1)}, u32[]{:S(2)}, u32[]{:S(2)}) %all-to-all-start) | async-done | bytes 131104 | tf_op jit(solution)/shard_map/all_to_all | solution.py:178
  92.7 3.3 %all-to-all-start.2 = ((bf16[128,4,128]{2,0,1:T(8,128)(2,1)}), bf16[128,4,128]{2,0,1:T(8,128)(2,1)S(1)}, u32[]{:S(2)}, u32[]{:S(2)}) async-start(bf16[128,4,128]{2,0,1:T(8,128)(2,1)} %copy.48), calls=%async_computation.2 | async-start | bytes 262144 | tf_op jit(solution)/shard_map/all_to_all | solution.py:179
  99.0 1.2 copy.60
  100.2 1.8 all-to-all-done.2
  101.9 3.5 %all-to-all-start.7 = ((bf16[512,4,128]{2,1,0:T(4,128)(2,1)}), bf16[512,4,128]{2,1,0:T(4,128)(2,1)S(1)}, u32[]{:S(2)}, u32[]{:S(2)}) async-start(bf16[512,4,128]{2,1,0:T(4,128)(2,1)} %copy.60), calls=%async_computation.7 | async-start | bytes 1048576 | tf_op jit(solution)/shard_map/all_to_all | solution.py:202
  105.4 3.9 %fusion.12 = (f32[4,512]{1,0:T(4,128)S(1)}, bf16[4,512,128]{2,1,0:T(8,128)(2,1)S(1)}) fusion(bf16[4,128,4,128]{3,1,0,2:T(8,128)(2,1)S(1)} %copy.54, bf16[512,128]{1,0:T(8,128)(2,1)S(1)} %bitcast.111, f32[4,512,512]{2,1,0:T(8,128)} %copy-done.1, f32[4,512]{1,0:T(4,128)S(1)} %log_add_fusion, pred[512,512]{0,1:T(8,128)(4,1)S(1)} %fusion.13), kind=kOutput, calls=%fused_computation.24 | convolution fusion | flops 273938432 | bytes 5652480 | tf_op jit(solution)/shard_map/while/body/eval_jaxpr/while/body/hqk,khd->qhd/dot_general | solution.py:74
  109.3 1.4 fusion
  112.1 1.2 copy.58
  113.3 5.2 %all-to-all-done.7 = bf16[512,4,128]{2,1,0:T(4,128)(2,1)S(1)} async-done(((bf16[512,4,128]{2,1,0:T(4,128)(2,1)}), bf16[512,4,128]{2,1,0:T(4,128)(2,1)S(1)}, u32[]{:S(2)}, u32[]{:S(2)}) %all-to-all-start.7) | async-done | bytes 524320 | tf_op jit(solution)/shard_map/all_to_all | solution.py:202
  118.5 3.5 %all-to-all-start.6 = ((bf16[512,4,128]{2,1,0:T(4,128)(2,1)}), bf16[512,4,128]{2,1,0:T(4,128)(2,1)S(1)}, u32[]{:S(2)}, u32[]{:S(2)}) async-start(bf16[512,4,128]{2,1,0:T(4,128)(2,1)} %copy.58), calls=%async_computation.6 | async-start | bytes 1048576 | tf_op jit(solution)/shard_map/all_to_all | solution.py:201
  123.0 12.3 %all-to-all-done.6 = bf16[512,4,128]{2,1,0:T(4,128)(2,1)S(1)} async-done(((bf16[512,4,128]{2,1,0:T(4,128)(2,1)}), bf16[512,4,128]{2,1,0:T(4,128)(2,1)S(1)}, u32[]{:S(2)}, u32[]{:S(2)}) %all-to-all-start.6) | async-done | bytes 524320 | tf_op jit(solution)/shard_map/all_to_all | solution.py:201
  136.1 3.2 %convert_bitcast_fusion = bf16[2048,1024]{0,1:T(8,128)(2,1)} fusion(bf16[1,128,2048]{2,1,0:T(8,128)(2,1)S(1)} %copy-done, bf16[128,512]{0,1:T(8,128)(2,1)S(1)} %bitcast.98, bf16[128,512]{0,1:T(8,128)(2,1)S(1)} %bitcast.100), kind=kOutput, calls=%fused_computation.6 | convolution fusion | flops 539492352 | bytes 4980736 | tf_op jit(solution)/shard_map/dot_general | solution.py:226
  139.4 1.2 copy.50
  140.6 3.5 %all-to-all-start.3 = ((bf16[512,4,128]{2,1,0:T(4,128)(2,1)}), bf16[512,4,128]{2,1,0:T(4,128)(2,1)S(1)}, u32[]{:S(2)}, u32[]{:S(2)}) async-start(bf16[512,4,128]{2,1,0:T(4,128)(2,1)} %copy.50), calls=%async_computation.3 | async-start | bytes 1048576 | tf_op jit(solution)/shard_map/all_to_all | solution.py:186
  145.0 1.2 copy.56
  146.2 19.1 %all-to-all-done.3 = bf16[512,4,128]{2,1,0:T(4,128)(2,1)S(1)} async-done(((bf16[512,4,128]{2,1,0:T(4,128)(2,1)}), bf16[512,4,128]{2,1,0:T(4,128)(2,1)S(1)}, u32[]{:S(2)}, u32[]{:S(2)}) %all-to-all-start.3) | async-done | bytes 524320 | tf_op jit(solution)/shard_map/all_to_all | solution.py:186
  165.3 4.3 %all-to-all-start.5 = ((bf16[512,4,128]{2,1,0:T(4,128)(2,1)}), bf16[512,4,128]{2,1,0:T(4,128)(2,1)S(1)}, u32[]{:S(2)}, u32[]{:S(2)}) async-start(bf16[512,4,128]{2,1,0:T(4,128)(2,1)} %copy.56), calls=%async_computation.5 | async-start | bytes 1048576 | tf_op jit(solution)/shard_map/all_to_all | solution.py:200
  169.6 34.6 %reduce-scatter.2.cloned.1.call-done = bf16[256,1024]{0,1:T(8,128)(2,1)} async-done(((bf16[2048,1024]{0,1:T(8,128)(2,1)}), bf16[256,1024]{0,1:T(8,128)(2,1)}) %reduce-scatter.2.cloned.1.call-update) | async-done | bytes 524304 | tf_op jit(solution)/shard_map/reduce_scatter | solution.py:225
  204.4 1.2 reshape.232
  205.8 1.2 reshape.233
  207.0 4.5 %fusion.5 = bf16[1,128,2048]{2,1,0:T(8,128)(2,1)} fusion(bf16[2048,1024]{1,0:T(8,128)(2,1)} %all-gather.3.cloned.1.call-done, bf16[128,512]{0,1:T(8,128)(2,1)S(1)} %bitcast.99, bf16[128,512]{0,1:T(8,128)(2,1)S(1)} %bitcast.101), kind=kOutput, calls=%fused_computation.11 | convolution fusion | flops 537657344 | bytes 4980736 | tf_op jit(solution)/shard_map/dot_general | solution.py:217
  211.5 27.7 %all-reduce.2.cloned.1.call-done = bf16[256,1024]{0,1:T(8,128)(2,1)} async-done(((bf16[256,1024]{0,1:T(8,128)(2,1)}), bf16[256,1024]{0,1:T(8,128)(2,1)}) %all-reduce.2.cloned.1.call-update) | async-done | bytes 524304 | tf_op jit(solution)/shard_map/psum | solution.py:233
  (42 shorter events, 12.5 us)
Async XLA Ops:
  7.2 71.5 %copy-start = (bf16[1,128,2048]{2,1,0:T(8,128)(2,1)S(1)}, bf16[1,128,2048]{2,1,0:T(8,128)(2,1)}, u32[]{:S(2)}) copy-start(bf16[1,128,2048]{2,1,0:T(8,128)(2,1)} %param.6) | copy-start | bytes 1572868
  7.2 40.7 %copy-start.3 = (s32[1,128]{1,0:T(1,128)S(1)}, s32[1,128]{1,0:T(1,128)}, u32[]{:S(2)}) copy-start(s32[1,128]{1,0:T(1,128)} %param.10) | copy-start | bytes 1540
  7.2 71.5 %all-gather.3.cloned.1.call-start = ((), (), s32[]{:S(2)}) async-start(), calls=%async_computation.9 | async-start | bytes 4718592 | tf_op jit(solution)/shard_map/all_gather | solution.py:163
  11.2 33.0 %all-to-all-start.1 = ((bf16[128,16,128]{0,2,1:T(8,128)(2,1)}), bf16[128,16,128]{0,2,1:T(8,128)(2,1)S(1)}, u32[]{:S(2)}, u32[]{:S(2)}) async-start(bf16[128,16,128]{0,2,1:T(8,128)(2,1)} %bitcast.9), calls=%async_computation.1 | async-start | bytes 1048576 | tf_op jit(solution)/shard_map/all_to_all | solution.py:177
  44.2 38.7 %all-to-all-start.4 = ((bf16[128,16,128]{0,2,1:T(8,128)(2,1)}), bf16[128,16,128]{0,2,1:T(8,128)(2,1)S(1)}, u32[]{:S(2)}, u32[]{:S(2)}) async-start(bf16[128,16,128]{0,2,1:T(8,128)(2,1)} %bitcast.22), calls=%async_computation.4 | async-start | bytes 1048576 | tf_op jit(solution)/shard_map/all_to_all | solution.py:189
  83.0 9.7 %all-to-all-start = ((bf16[128,4,128]{2,0,1:T(8,128)(2,1)}), bf16[128,4,128]{2,0,1:T(8,128)(2,1)S(1)}, u32[]{:S(2)}, u32[]{:S(2)}) async-start(bf16[128,4,128]{2,0,1:T(8,128)(2,1)} %copy.44), calls=%async_computation | async-start | bytes 262144 | tf_op jit(solution)/shard_map/all_to_all | solution.py:178
  92.7 9.2 %all-to-all-start.2 = ((bf16[128,4,128]{2,0,1:T(8,128)(2,1)}), bf16[128,4,128]{2,0,1:T(8,128)(2,1)S(1)}, u32[]{:S(2)}, u32[]{:S(2)}) async-start(bf16[128,4,128]{2,0,1:T(8,128)(2,1)} %copy.48), calls=%async_computation.2 | async-start | bytes 262144 | tf_op jit(solution)/shard_map/all_to_all | solution.py:179
  96.9 2.0 copy-start.1
  101.9 16.6 %all-to-all-start.7 = ((bf16[512,4,128]{2,1,0:T(4,128)(2,1)}), bf16[512,4,128]{2,1,0:T(4,128)(2,1)S(1)}, u32[]{:S(2)}, u32[]{:S(2)}) async-start(bf16[512,4,128]{2,1,0:T(4,128)(2,1)} %copy.60), calls=%async_computation.7 | async-start | bytes 1048576 | tf_op jit(solution)/shard_map/all_to_all | solution.py:202
  105.4 3.9 %copy-start.2 = (f32[4,512,512]{2,1,0:T(8,128)S(1)}, f32[4,512,512]{2,1,0:T(8,128)}, u32[]{:S(2)}) copy-start(f32[4,512,512]{2,1,0:T(8,128)} %copy-done.1) | copy-start | bytes 12582916
  110.7 1.4 copy-start.4
  118.5 16.8 %all-to-all-start.6 = ((bf16[512,4,128]{2,1,0:T(4,128)(2,1)}), bf16[512,4,128]{2,1,0:T(4,128)(2,1)S(1)}, u32[]{:S(2)}, u32[]{:S(2)}) async-start(bf16[512,4,128]{2,1,0:T(4,128)(2,1)} %copy.58), calls=%async_computation.6 | async-start | bytes 1048576 | tf_op jit(solution)/shard_map/all_to_all | solution.py:201
  122.0 82.2 %reduce-scatter.2.cloned.1.call-start = ((), (), s32[]{:S(2)}) async-start(), calls=%async_computation.10 | async-start | bytes 4718592 | tf_op jit(solution)/shard_map/reduce_scatter | solution.py:225
  139.3 4.7 %copy-start.5 = (bf16[4,512,512]{1,2,0:T(8,128)(2,1)S(1)}, bf16[4,512,512]{1,2,0:T(8,128)(2,1)}, u32[]{:S(2)}) copy-start(bf16[4,512,512]{1,2,0:T(8,128)(2,1)} %copy-done.4) | copy-start | bytes 6291460
  140.6 24.7 %all-to-all-start.3 = ((bf16[512,4,128]{2,1,0:T(4,128)(2,1)}), bf16[512,4,128]{2,1,0:T(4,128)(2,1)S(1)}, u32[]{:S(2)}, u32[]{:S(2)}) async-start(bf16[512,4,128]{2,1,0:T(4,128)(2,1)} %copy.50), calls=%async_computation.3 | async-start | bytes 1048576 | tf_op jit(solution)/shard_map/all_to_all | solution.py:186
  165.3 40.3 %all-to-all-start.5 = ((bf16[512,4,128]{2,1,0:T(4,128)(2,1)}), bf16[512,4,128]{2,1,0:T(4,128)(2,1)S(1)}, u32[]{:S(2)}, u32[]{:S(2)}) async-start(bf16[512,4,128]{2,1,0:T(4,128)(2,1)} %copy.56), calls=%async_computation.5 | async-start | bytes 1048576 | tf_op jit(solution)/shard_map/all_to_all | solution.py:200
  169.6 69.6 %all-reduce.2.cloned.1.call-start = ((), (), s32[]{:S(2)}) async-start(), calls=%async_computation.11 | async-start | bytes 1048576 | tf_op jit(solution)/shard_map/psum | solution.py:233
Sparse Core Ops, SparseCore 0:
  10.2 68.4 all-gather.2
  139.5 64.6 reduce-scatter.1
  206.5 32.6 all-reduce.1
where the time goes:
time: 249 us; the launch traced here: 248 us
  waiting for transfers between devices  139 us (56%)
  starting transfers between devices  31.6 us (13%)
  blocking collectives  21.7 us (9%)
  matrix products  19.9 us (8%)
  local copies, waits for them, and re-layouts  17.4 us (7%)
  between operations  14 us (6%)
  other arithmetic  4.52 us (2%)
    reduce_scatter x1, waiting for transfers between devices, body(): lax.psum_scatter(lax.dot_general(columns, grad_kv, (((0,), (0,)), ((), ()...  34.6 us
    psum x1, waiting for transfers between devices, body(): grad_total = lax.psum(grad_shard, 'rep').astype(jnp.bfloat16)  27.7 us
    all_to_all x1, waiting for transfers between devices, body(): lax.all_to_all(sent[0], 'seq', split_axis=1, concat_axis=0, tiled=True)  24.7 us
    all_gather x1, blocking collectives, body(): seg_all = lax.all_gather(segment_ids[0], 'seq', axis=0, tiled=True)  21.7 us
    all_to_all x1, waiting for transfers between devices, body(): lax.all_to_all(out_part, 'seq', split_axis=0, concat_axis=1, tiled=True)  19.1 us
    all_to_all x1, waiting for transfers between devices, body(): lax.all_to_all(key_back, 'seq', split_axis=0, concat_axis=1, tiled=True)  12.3 us
    all_gather x1, waiting for transfers between devices, body(): lax.all_gather(stacked, ('seq', 'fsdp'), axis=0, tiled=True)  9.14 us
    unnamed x16, local copies, waits for them, and re-layouts  6.44 us
  transfers between devices with their start and end apart: 11, of which 9 were waited for; matrix products, arithmetic and copies ran while one was open for 13% of the time, Pallas kernels for 0%

commit v1 on v0

--- a/solution.py
+++ b/solution.py
@@ -8,6 +8,29 @@
 KV_HEADS = 4
 HEAD_DIM = 128
 masked_low = -1e30
+
+
+def split_up(x, dim, length):
+    before, after = (x.shape[:dim], x.shape[dim + 1 :])
+    return jnp.moveaxis(x.reshape(*before, length, -1, *after), dim, 0)
+
+
+def joined_along(blocks, dim):
+    lengths = list(blocks.shape[1:])
+    lengths[dim] *= blocks.shape[0]
+    return jnp.moveaxis(blocks, 0, dim).reshape(lengths)
+
+
+def rotated_exchange(x, axis, split_dim, concat_dim):
+    length, index = (lax.axis_size(axis), lax.axis_index(axis))
+    blocks = split_up(x, split_dim, length)
+    result = blocks
+    for step in range(1, length):
+        target, source = ((index + step) % length, (index - step) % length)
+        sent = lax.dynamic_index_in_dim(blocks, target, 0)
+        other = lax.ppermute(sent, axis, [(i, (i + step) % length) for i in range(length)])
+        result = lax.dynamic_update_slice_in_dim(result, other, source, axis=0)
+    return joined_along(result, concat_dim)
 
 
 def block_mask(seg_all, row_start, col_start, block_width):
@@ -174,7 +197,7 @@
         jnp.repeat(value_rows, kv_copies, axis=1),
     )
     query_part, key_part, value_part = (
-        lax.all_to_all(sent[0], "seq", split_axis=1, concat_axis=0, tiled=True),
+        rotated_exchange(sent[0], "seq", 1, 0),
         lax.all_to_all(sent[1], "seq", split_axis=1, concat_axis=0, tiled=True),
         lax.all_to_all(sent[2], "seq", split_axis=1, concat_axis=0, tiled=True),
     )

time: 249 us -> 245 us (0.984)
  waiting for transfers between devices: 139 us -> 126 us
  blocking collectives: 21.7 us -> 28.2 us
    all_to_all x1 -> x0, waiting for transfers between devices: 24.7 us -> none  [body(): lax.all_to_all(sent[0], 'seq', split_axis=1, concat_axis=0, tiled=True)]
    all_gather x1, waiting for transfers between devices: 9.14 us -> 22.2 us  [body(): lax.all_gather(stacked, ('seq', 'fsdp'), axis=0, tiled=True)]
    all_gather x1, blocking collectives: 21.7 us -> 28.2 us  [body(): seg_all = lax.all_gather(segment_ids[0], 'seq', axis=0, tiled=True)]
    all_to_all x1 -> x0, starting transfers between devices: 6.32 us -> none  [body(): lax.all_to_all(sent[0], 'seq', split_axis=1, concat_axis=0, tiled=True)]
    ppermute x0 -> x3, starting transfers between devices: none -> 6.11 us  [rotated_exchange(): lax.ppermute(sent, axis, [(i, (i + step) % length) for i in range(length)])]
    unnamed x16 -> x13, local copies, waits for them, and re-layouts: 6.44 us -> 4.39 us
  transfers between devices with their start and end apart: 11 -> 13, of which waited for: 9 -> 8; matrix products, arithmetic and copies ran while one was open for 13% -> 14% of each run, Pallas kernels for 0% -> 0%
where the time goes in v1:
time: 245 us; the launch traced here: 244 us
  waiting for transfers between devices  126 us (51%)
  starting transfers between devices  32.8 us (13%)
  blocking collectives  28.2 us (12%)
  matrix products  21.7 us (9%)
  local copies, waits for them, and re-layouts  17.1 us (7%)
  between operations  14.1 us (6%)
  other arithmetic  4.52 us (2%)
    reduce_scatter x1, waiting for transfers between devices, body(): lax.psum_scatter(lax.dot_general(columns, grad_kv, (((0,), (0,)), ((), ()...  34.9 us
    all_gather x1, blocking collectives, body(): seg_all = lax.all_gather(segment_ids[0], 'seq', axis=0, tiled=True)  28.2 us
    psum x1, waiting for transfers between devices, body(): grad_total = lax.psum(grad_shard, 'rep').astype(jnp.bfloat16)  28 us
    all_gather x1, waiting for transfers between devices, body(): lax.all_gather(stacked, ('seq', 'fsdp'), axis=0, tiled=True)  22.2 us
    all_to_all x1, waiting for transfers between devices, body(): lax.all_to_all(out_part, 'seq', split_axis=0, concat_axis=1, tiled=True)  16.9 us
    all_to_all x1, waiting for transfers between devices, body(): lax.all_to_all(key_back, 'seq', split_axis=0, concat_axis=1, tiled=True)  12.1 us
    ppermute x3, starting transfers between devices, rotated_exchange(): lax.ppermute(sent, axis, [(i, (i + step) % length) for i in range(length)])  6.11 us
    all_to_all x1, waiting for transfers between devices, body(): lax.all_to_all(value_back, 'seq', split_axis=0, concat_axis=1, tiled=True)  5.02 us
  transfers between devices with their start and end apart: 13, of which 8 were waited for; matrix products, arithmetic and copies ran while one was open for 14% of the time, Pallas kernels for 0%

profile of v1, /device:TPU:0, one launch (start us, length us, event | category | flops | bytes accessed | tf_op | source)
XLA Modules:
  0.0 244.3 jit_solution(13120320076566524262)
XLA Ops:
  7.2 1.9 pad_maximum_fusion
  9.2 1.4 reshape_reshape_squeeze.3
  10.8 5.1 %collective-permute-start.2 = (bf16[1,128,4,128]{3,2,0,1:T(4,128)(2,1)S(1)}, bf16[1,128,4,128]{3,2,0,1:T(4,128)(2,1)S(1)}, u32[]{:S(2)}, u32[]{:S(2)}) collective-permute-start(bf16[1,128,4,128]{3,2,0,1:T(4,128)(2,1)S(1)} %get-tuple-element.282), channel_id=1, source_target_pairs={{0,12},{4,0},{8,4},{12,8},{1,13},{5,1},{9,5},{13,9},{2,14},{6,2},{... | collective-permute-start | bytes 393224 | tf_op jit(solution)/shard_map/ppermute | solution.py:31
  16.9 2.0 copy.49
  19.0 4.1 %all-to-all-start.3 = ((bf16[128,16,128]{0,2,1:T(8,128)(2,1)}), bf16[128,16,128]{0,2,1:T(8,128)(2,1)S(1)}, u32[]{:S(2)}, u32[]{:S(2)}) async-start(bf16[128,16,128]{0,2,1:T(8,128)(2,1)} %bitcast.21), calls=%async_computation.3 | async-start | bytes 1048576 | tf_op jit(solution)/shard_map/all_to_all | solution.py:212
  23.1 28.2 %all-gather = s32[1,512]{1,0:T(1,128)S(1)} all-gather(s32[1,128]{1,0:T(1,128)S(1)} %copy-done.3), channel_id=2, replica_groups=mesh['groups'=2,'seq'=4,'rep'=2,'fsdp'=2] {'seq'}, dimensions={1}, use_global_device_ids=true | all-gather | bytes 2560 | tf_op jit(solution)/shard_map/all_gather | solution.py:207
  51.6 22.2 %all-gather.3.cloned.1.call-done = bf16[2048,1024]{1,0:T(8,128)(2,1)} async-done(((bf16[256,1024]{1,0:T(8,128)(2,1)}), bf16[2048,1024]{1,0:T(8,128)(2,1)}) %all-gather.3.cloned.1.call-update) | async-done | bytes 4194320 | tf_op jit(solution)/shard_map/all_gather | solution.py:186
  73.8 3.5 %fusion.8 = bf16[128,1024]{0,1:T(8,128)(2,1)S(1)} fusion(bf16[2048,1024]{1,0:T(8,128)(2,1)} %all-gather.3.cloned.1.call-done, bf16[1,128,2048]{2,1,0:T(8,128)(2,1)S(1)} %copy-done), kind=kOutput, calls=%fused_computation.19 | convolution fusion | flops 537001984 | bytes 4980736 | tf_op jit(solution)/shard_map/dot_general | solution.py:184
  78.1 4.7 %all-to-all-start = ((bf16[128,4,128]{2,0,1:T(8,128)(2,1)}), bf16[128,4,128]{2,0,1:T(8,128)(2,1)S(1)}, u32[]{:S(2)}, u32[]{:S(2)}) async-start(bf16[128,4,128]{2,0,1:T(8,128)(2,1)} %copy.44), calls=%async_computation | async-start | bytes 262144 | tf_op jit(solution)/shard_map/all_to_all | solution.py:201
  84.2 4.9 %all-to-all-done = bf16[128,4,128]{2,0,1:T(8,128)(2,1)S(1)} async-done(((bf16[128,4,128]{2,0,1:T(8,128)(2,1)}), bf16[128,4,128]{2,0,1:T(8,128)(2,1)S(1)}, u32[]{:S(2)}, u32[]{:S(2)}) %all-to-all-start) | async-done | bytes 131104 | tf_op jit(solution)/shard_map/all_to_all | solution.py:201
  89.1 3.3 %all-to-all-start.1 = ((bf16[128,4,128]{2,0,1:T(8,128)(2,1)}), bf16[128,4,128]{2,0,1:T(8,128)(2,1)S(1)}, u32[]{:S(2)}, u32[]{:S(2)}) async-start(bf16[128,4,128]{2,0,1:T(8,128)(2,1)} %copy.45), calls=%async_computation.1 | async-start | bytes 262144 | tf_op jit(solution)/shard_map/all_to_all | solution.py:202
  95.4 1.2 copy.57
  96.6 1.8 all-to-all-done.1
  98.3 3.5 %all-to-all-start.6 = ((bf16[512,4,128]{2,1,0:T(4,128)(2,1)}), bf16[512,4,128]{2,1,0:T(4,128)(2,1)S(1)}, u32[]{:S(2)}, u32[]{:S(2)}) async-start(bf16[512,4,128]{2,1,0:T(4,128)(2,1)} %copy.57), calls=%async_computation.6 | async-start | bytes 1048576 | tf_op jit(solution)/shard_map/all_to_all | solution.py:225
  101.8 3.9 %fusion.9 = (f32[4,512]{1,0:T(4,128)S(1)}, bf16[4,512,128]{2,1,0:T(8,128)(2,1)S(1)}) fusion(bf16[4,128,4,128]{3,1,0,2:T(8,128)(2,1)S(1)} %copy.51, bf16[512,128]{1,0:T(8,128)(2,1)S(1)} %bitcast.95, f32[4,512,512]{1,2,0:T(8,128)} %copy-done.1, f32[4,512]{1,0:T(4,128)S(1)} %log_add_fusion, pred[512,512]{0,1:T(8,128)(4,1)S(1)} %fusion.10), kind=kOutput, calls=%fused_computation.21 | convolution fusion | flops 273938432 | bytes 5652480 | tf_op jit(solution)/shard_map/while/body/eval_jaxpr/while/body/hqk,khd->qhd/dot_general | solution.py:97
  105.7 1.5 fusion
  108.5 1.2 copy.55
  109.7 5.0 %all-to-all-done.6 = bf16[512,4,128]{2,1,0:T(4,128)(2,1)S(1)} async-done(((bf16[512,4,128]{2,1,0:T(4,128)(2,1)}), bf16[512,4,128]{2,1,0:T(4,128)(2,1)S(1)}, u32[]{:S(2)}, u32[]{:S(2)}) %all-to-all-start.6) | async-done | bytes 524320 | tf_op jit(solution)/shard_map/all_to_all | solution.py:225
  114.8 3.5 %all-to-all-start.5 = ((bf16[512,4,128]{2,1,0:T(4,128)(2,1)}), bf16[512,4,128]{2,1,0:T(4,128)(2,1)S(1)}, u32[]{:S(2)}, u32[]{:S(2)}) async-start(bf16[512,4,128]{2,1,0:T(4,128)(2,1)} %copy.55), calls=%async_computation.5 | async-start | bytes 1048576 | tf_op jit(solution)/shard_map/all_to_all | solution.py:224
  119.3 12.1 %all-to-all-done.5 = bf16[512,4,128]{2,1,0:T(4,128)(2,1)S(1)} async-done(((bf16[512,4,128]{2,1,0:T(4,128)(2,1)}), bf16[512,4,128]{2,1,0:T(4,128)(2,1)S(1)}, u32[]{:S(2)}, u32[]{:S(2)}) %all-to-all-start.5) | async-done | bytes 524320 | tf_op jit(solution)/shard_map/all_to_all | solution.py:224
  132.2 3.2 %convert_bitcast_fusion = bf16[2048,1024]{0,1:T(8,128)(2,1)} fusion(bf16[1,128,2048]{2,1,0:T(8,128)(2,1)S(1)} %copy-done, bf16[128,512]{0,1:T(8,128)(2,1)S(1)} %bitcast.82, bf16[128,512]{0,1:T(8,128)(2,1)S(1)} %bitcast.84), kind=kOutput, calls=%fused_computation.2 | convolution fusion | flops 539492352 | bytes 4980736 | tf_op jit(solution)/shard_map/dot_general | solution.py:249
  135.4 1.2 copy.47
  136.6 3.5 %all-to-all-start.2 = ((bf16[512,4,128]{2,1,0:T(4,128)(2,1)}), bf16[512,4,128]{2,1,0:T(4,128)(2,1)S(1)}, u32[]{:S(2)}, u32[]{:S(2)}) async-start(bf16[512,4,128]{2,1,0:T(4,128)(2,1)} %copy.47), calls=%async_computation.2 | async-start | bytes 1048576 | tf_op jit(solution)/shard_map/all_to_all | solution.py:209
  140.1 2.6 %fusion.6 = bf16[512,4,128]{2,0,1:T(8,128)(2,1)S(1)} fusion(bf16[4,512,512]{1,2,0:T(8,128)(2,1)} %copy-done.4, bf16[512,128]{1,0:T(8,128)(2,1)S(1)} %bitcast.87), kind=kOutput, calls=%fused_computation.16 | convolution fusion | flops 268959744 | bytes 2752512 | tf_op jit(solution)/shard_map/while/body/eval_jaxpr/while/body/hqk,khd->qhd/dot_general | solution.py:149
  142.7 1.2 copy.53
  143.9 16.9 %all-to-all-done.2 = bf16[512,4,128]{2,1,0:T(4,128)(2,1)S(1)} async-done(((bf16[512,4,128]{2,1,0:T(4,128)(2,1)}), bf16[512,4,128]{2,1,0:T(4,128)(2,1)S(1)}, u32[]{:S(2)}, u32[]{:S(2)}) %all-to-all-start.2) | async-done | bytes 524320 | tf_op jit(solution)/shard_map/all_to_all | solution.py:209
  160.9 4.0 %all-to-all-start.4 = ((bf16[512,4,128]{2,1,0:T(4,128)(2,1)}), bf16[512,4,128]{2,1,0:T(4,128)(2,1)S(1)}, u32[]{:S(2)}, u32[]{:S(2)}) async-start(bf16[512,4,128]{2,1,0:T(4,128)(2,1)} %copy.53), calls=%async_computation.4 | async-start | bytes 1048576 | tf_op jit(solution)/shard_map/all_to_all | solution.py:223
  164.8 34.9 %reduce-scatter.2.cloned.1.call-done = bf16[256,1024]{0,1:T(8,128)(2,1)} async-done(((bf16[2048,1024]{0,1:T(8,128)(2,1)}), bf16[256,1024]{0,1:T(8,128)(2,1)}) %reduce-scatter.2.cloned.1.call-update) | async-done | bytes 524304 | tf_op jit(solution)/shard_map/reduce_scatter | solution.py:248
  199.9 1.2 reshape.239
  201.3 1.2 reshape.240
  202.5 4.5 %fusion.2 = bf16[1,128,2048]{2,1,0:T(8,128)(2,1)} fusion(bf16[2048,1024]{1,0:T(8,128)(2,1)} %all-gather.3.cloned.1.call-done, bf16[128,512]{0,1:T(8,128)(2,1)S(1)} %bitcast.83, bf16[128,512]{0,1:T(8,128)(2,1)S(1)} %bitcast.85), kind=kOutput, calls=%fused_computation.8 | convolution fusion | flops 537657344 | bytes 4980736 | tf_op jit(solution)/shard_map/dot_general | solution.py:240
  207.0 28.0 %all-reduce.2.cloned.1.call-done = bf16[256,1024]{0,1:T(8,128)(2,1)} async-done(((bf16[256,1024]{0,1:T(8,128)(2,1)}), bf16[256,1024]{0,1:T(8,128)(2,1)}) %all-reduce.2.cloned.1.call-update) | async-done | bytes 524304 | tf_op jit(solution)/shard_map/psum | solution.py:256
  (48 shorter events, 12.9 us)
Async XLA Ops:
  7.2 66.7 %copy-start = (bf16[1,128,2048]{2,1,0:T(8,128)(2,1)S(1)}, bf16[1,128,2048]{2,1,0:T(8,128)(2,1)}, u32[]{:S(2)}) copy-start(bf16[1,128,2048]{2,1,0:T(8,128)(2,1)} %param.6) | copy-start | bytes 1572868
  7.2 15.9 %copy-start.3 = (s32[1,128]{1,0:T(1,128)S(1)}, s32[1,128]{1,0:T(1,128)}, u32[]{:S(2)}) copy-start(s32[1,128]{1,0:T(1,128)} %param.10) | copy-start | bytes 1540
  7.2 66.6 %all-gather.3.cloned.1.call-start = ((), (), s32[]{:S(2)}) async-start(), calls=%async_computation.8 | async-start | bytes 4718592 | tf_op jit(solution)/shard_map/all_gather | solution.py:186
  10.8 72.1 %collective-permute-start.2 = (bf16[1,128,4,128]{3,2,0,1:T(4,128)(2,1)S(1)}, bf16[1,128,4,128]{3,2,0,1:T(4,128)(2,1)S(1)}, u32[]{:S(2)}, u32[]{:S(2)}) collective-permute-start(bf16[1,128,4,128]{3,2,0,1:T(4,128)(2,1)S(1)} %get-tuple-element.282), channel_id=1, source_target_pairs={{0,12},{4,0},{8,4},{12,8},{1,13},{5,1},{9,5},{13,9},{2,14},{6,2},{... | collective-permute-start | bytes 393224 | tf_op jit(solution)/shard_map/ppermute | solution.py:31
  15.9 66.9 %collective-permute-start.1 = (bf16[1,128,4,128]{3,2,0,1:T(4,128)(2,1)S(1)}, bf16[1,128,4,128]{3,2,0,1:T(4,128)(2,1)S(1)}, u32[]{:S(2)}, u32[]{:S(2)}) collective-permute-start(bf16[1,128,4,128]{3,2,0,1:T(4,128)(2,1)S(1)} %get-tuple-element.283), channel_id=1, source_target_pairs={{0,8},{4,12},{8,0},{12,4},{1,9},{5,13},{9,1},{13,5},{2,10},{6,14},... | collective-permute-start | bytes 393224 | tf_op jit(solution)/shard_map/ppermute | solution.py:31
  15.9 35.6 %collective-permute-start = (bf16[1,128,4,128]{3,2,0,1:T(4,128)(2,1)S(1)}, bf16[1,128,4,128]{3,2,0,1:T(4,128)(2,1)S(1)}, u32[]{:S(2)}, u32[]{:S(2)}) collective-permute-start(bf16[1,128,4,128]{3,2,0,1:T(4,128)(2,1)S(1)} %get-tuple-element.284), channel_id=1, source_target_pairs={{0,4},{4,8},{8,12},{12,0},{1,5},{5,9},{9,13},{13,1},{2,6},{6,10},{... | collective-permute-start | bytes 393224 | tf_op jit(solution)/shard_map/ppermute | solution.py:31
  19.0 59.2 %all-to-all-start.3 = ((bf16[128,16,128]{0,2,1:T(8,128)(2,1)}), bf16[128,16,128]{0,2,1:T(8,128)(2,1)S(1)}, u32[]{:S(2)}, u32[]{:S(2)}) async-start(bf16[128,16,128]{0,2,1:T(8,128)(2,1)} %bitcast.21), calls=%async_computation.3 | async-start | bytes 1048576 | tf_op jit(solution)/shard_map/all_to_all | solution.py:212
  78.1 11.0 %all-to-all-start = ((bf16[128,4,128]{2,0,1:T(8,128)(2,1)}), bf16[128,4,128]{2,0,1:T(8,128)(2,1)S(1)}, u32[]{:S(2)}, u32[]{:S(2)}) async-start(bf16[128,4,128]{2,0,1:T(8,128)(2,1)} %copy.44), calls=%async_computation | async-start | bytes 262144 | tf_op jit(solution)/shard_map/all_to_all | solution.py:201
  89.1 9.2 %all-to-all-start.1 = ((bf16[128,4,128]{2,0,1:T(8,128)(2,1)}), bf16[128,4,128]{2,0,1:T(8,128)(2,1)S(1)}, u32[]{:S(2)}, u32[]{:S(2)}) async-start(bf16[128,4,128]{2,0,1:T(8,128)(2,1)} %copy.45), calls=%async_computation.1 | async-start | bytes 262144 | tf_op jit(solution)/shard_map/all_to_all | solution.py:202
  93.3 2.0 copy-start.1
  98.3 16.4 %all-to-all-start.6 = ((bf16[512,4,128]{2,1,0:T(4,128)(2,1)}), bf16[512,4,128]{2,1,0:T(4,128)(2,1)S(1)}, u32[]{:S(2)}, u32[]{:S(2)}) async-start(bf16[512,4,128]{2,1,0:T(4,128)(2,1)} %copy.57), calls=%async_computation.6 | async-start | bytes 1048576 | tf_op jit(solution)/shard_map/all_to_all | solution.py:225
  101.8 3.9 %copy-start.2 = (f32[4,512,512]{1,2,0:T(8,128)S(1)}, f32[4,512,512]{1,2,0:T(8,128)}, u32[]{:S(2)}) copy-start(f32[4,512,512]{1,2,0:T(8,128)} %copy-done.1) | copy-start | bytes 12582916
  107.2 1.4 copy-start.4
  114.8 16.6 %all-to-all-start.5 = ((bf16[512,4,128]{2,1,0:T(4,128)(2,1)}), bf16[512,4,128]{2,1,0:T(4,128)(2,1)S(1)}, u32[]{:S(2)}, u32[]{:S(2)}) async-start(bf16[512,4,128]{2,1,0:T(4,128)(2,1)} %copy.55), calls=%async_computation.5 | async-start | bytes 1048576 | tf_op jit(solution)/shard_map/all_to_all | solution.py:224
  118.2 81.5 %reduce-scatter.2.cloned.1.call-start = ((), (), s32[]{:S(2)}) async-start(), calls=%async_computation.9 | async-start | bytes 4718592 | tf_op jit(solution)/shard_map/reduce_scatter | solution.py:248
  136.6 24.3 %all-to-all-start.2 = ((bf16[512,4,128]{2,1,0:T(4,128)(2,1)}), bf16[512,4,128]{2,1,0:T(4,128)(2,1)S(1)}, u32[]{:S(2)}, u32[]{:S(2)}) async-start(bf16[512,4,128]{2,1,0:T(4,128)(2,1)} %copy.47), calls=%async_computation.2 | async-start | bytes 1048576 | tf_op jit(solution)/shard_map/all_to_all | solution.py:209
  160.9 40.3 %all-to-all-start.4 = ((bf16[512,4,128]{2,1,0:T(4,128)(2,1)}), bf16[512,4,128]{2,1,0:T(4,128)(2,1)S(1)}, u32[]{:S(2)}, u32[]{:S(2)}) async-start(bf16[512,4,128]{2,1,0:T(4,128)(2,1)} %copy.53), calls=%async_computation.4 | async-start | bytes 1048576 | tf_op jit(solution)/shard_map/all_to_all | solution.py:223
  164.8 70.2 %all-reduce.2.cloned.1.call-start = ((), (), s32[]{:S(2)}) async-start(), calls=%async_computation.10 | async-start | bytes 1048576 | tf_op jit(solution)/shard_map/psum | solution.py:256
Sparse Core Ops, SparseCore 0:
  10.2 63.5 all-gather.2
  135.5 64.1 reduce-scatter.1
  202.0 32.9 all-reduce.1
